TPU v7x, 512 devices: a whole 4x8x8 slice. The times are simulated.
512 devices in a mesh: chan: 128 (over z, y, core), win: 4 (over x).
Axes of the slice: x: 4, y: 8, z: 8, core: 2. Of those that a mesh axis runs over, the one named last changes fastest.
Arguments:
- receivers: bfloat16 [8, 1024, 512], P('win', 'chan'), may hold values from -6 to 6
- sources: bfloat16 [8, 32768, 512], P('win', 'chan'), may hold values from -6 to 6
- coupling: float32 [1024], P('chan')
- lag_basis: float32 [200, 32], replicated, may hold values from -0.4375 to 0.4375
- source_order: int32 [2], replicated, may hold values from 0 to 127
Outputs:
- gather_projections: float32 [2, 1024, 32, 256], P(None, 'chan', None, 'win')
Inputs may be any that keep to these rules, and one draw needn't show every extreme that they name: `source_order`: steps may name the same owner more than once.
All inputs are finite; a program needn't handle non-finite values.
Results may differ from a plain program's by a relative error of at most 0.0028.
Values may be sent and summed in bfloat16 or wider, within the bound.
A program may use at most 64 MiB of HBM per device.

v0:
```python
import functools
import math

import jax
import jax.numpy as jnp
from jax import lax
from jax.sharding import Mesh
from jax.sharding import PartitionSpec as P

CHAN = ("chan_0", "chan_1", "chan_2")


def from_root(block, axis, source):
    block = jnp.where(lax.axis_index(axis) == source, block, jnp.zeros_like(block))
    return lax.psum(block, axis)


def cut_along(shard, dim, size):
    before, after = (shard.shape[:dim], shard.shape[dim + 1 :])
    return jnp.moveaxis(shard.reshape(*before, size, -1, *after), dim, 0)


def sum_at_owner(shard, axis, dim):
    blocks = cut_along(shard, dim, lax.axis_size(axis))
    arrived = lax.all_to_all(blocks, axis, split_axis=0, concat_axis=0, tiled=True)
    return arrived.sum(axis=0)


def over_axes(shard, axes):
    return functools.reduce(lax.psum, axes, shard)


def phase_tables(band_size, lag_count):
    frequency = jnp.arange(band_size, dtype=jnp.int32)
    lag_shift = jnp.arange(lag_count, dtype=jnp.int32) - lag_count // 2
    phase_turns = frequency[:, None] * lag_shift[None, :] % (2 * band_size)
    phase = phase_turns.astype(jnp.float32) * (math.pi / band_size)
    return (jnp.cos(phase).T, jnp.sin(phase).T)


def twist(spectra, cosine_table, sine_table):
    band_size = spectra.shape[-1] // 2
    real_part = spectra[..., None, :band_size].astype(jnp.float32)
    imag_part = spectra[..., None, band_size:].astype(jnp.float32)
    twisted_real = real_part * cosine_table - imag_part * sine_table
    twisted_imag = real_part * sine_table + imag_part * cosine_table
    return jnp.concatenate([twisted_real, twisted_imag], axis=-1).astype(jnp.bfloat16)


def per_device(receivers, sources, coupling, lag_basis, source_order):
    window_count, chan_count, row_width = receivers.shape
    band_size = row_width // 2
    lag_count, basis_count = lag_basis.shape
    cosine_table, sine_table = phase_tables(band_size, lag_count)
    twisted = twist(receivers, cosine_table, sine_table).reshape(
        window_count, chan_count * lag_count, row_width
    )
    results = []
    for step_index in range(source_order.shape[0]):
        source_block = from_root(sources, CHAN, source_order[step_index])
        stacked = jnp.einsum(
            "wrf,wsf->rs", twisted, source_block, preferred_element_type=jnp.float32
        )
        gathers = stacked.reshape(chan_count, lag_count, -1) * coupling[:, None, None]
        projected_terms = jnp.einsum(
            "cls,lk->cks", gathers, lag_basis, precision=lax.Precision.HIGHEST
        )
        results.append(sum_at_owner(projected_terms, "win", 2))
    projections = jnp.stack(results)
    partial_power = jnp.sum(projections * projections, axis=(1, 2))
    power = over_axes(partial_power, CHAN) / (chan_count * lax.axis_size(CHAN) * basis_count)
    return projections * lax.rsqrt(power + 1e-05)[:, None, None, :]


def solution(mesh):
    split = Mesh(
        mesh.devices.reshape(8, 8, 2, mesh.shape["win"]), ("chan_0", "chan_1", "chan_2", "win")
    )
    placed = (P("win", CHAN, None), P("win", CHAN, None), P(CHAN), P(), P())
    return jax.shard_map(
        per_device,
        mesh=split,
        in_specs=placed,
        out_specs=P(None, CHAN, None, "win"),
        check_vma=False,
    )
```

profile of v0, /device:TPU:1, one launch (start us, length us, event | category | flops | bytes accessed | tf_op | source)
XLA Modules:
  0.0 291.4 jit_solution(5019641713420619160)
XLA Ops:
  6.5 1.4 fusion.25
  9.3 2.1 broadcast_select_fusion.1
  11.5 0.9 fusion.22
  12.4 0.1 mul.179
  12.5 0.1 mul.173
  12.6 0.9 fusion.1
  13.5 0.3 pad_maximum_fusion
  13.8 200.3 %all-reduce.3.cloned.1.call-done = (bf16[2,256,512]{2,1,0:T(8,128)(2,1)}, bf16[2,256,512]{2,1,0:T(8,128)(2,1)}) async-done(((bf16[2,256,512]{2,1,0:T(8,128)(2,1)}, bf16[2,256,512]{2,1,0:T(8,128)(2,1)}), (bf16[2,256,512]{2,1,0:T(8,128)(2,1)}, bf16[2,256,512]{2,1,0:T(8,128)(2,1)})) %all-reduce.3.cloned.1.call-update) | async-done | bytes 1048592 | tf_op jit(solution)/shard_map/psum | solution.py:15
  214.0 2.1 fusion.10
  216.2 1.8 fusion.7
  218.0 2.0 reshape.81
  220.0 1.9 copy.12
  221.9 2.1 reshape.87
  224.0 4.0 %all-to-all-start.1 = ((f32[4,1,16384]{2,1,0:T(1,128)}), f32[4,1,16384]{2,1,0:T(1,128)}, u32[]{:S(2)}, u32[]{:S(2)}) async-start(f32[4,1,16384]{2,1,0:T(1,128)} %reshape.87), calls=%async_computation.1 | async-start | bytes 524288 | tf_op jit(solution)/shard_map/all_to_all | solution.py:25
  228.1 2.1 fusion.12
  230.2 1.1 fusion.6
  231.3 0.2 reshape.80
  231.5 0.1 copy.13
  231.6 1.0 reshape.89
  232.6 1.0 all-to-all-done.1
  233.6 3.4 %all-to-all-start = ((f32[4,1,16384]{2,1,0:T(1,128)}), f32[4,1,16384]{2,1,0:T(1,128)S(1)}, u32[]{:S(2)}, u32[]{:S(2)}) async-start(f32[4,1,16384]{2,1,0:T(1,128)} %reshape.89), calls=%async_computation | async-start | bytes 524288 | tf_op jit(solution)/shard_map/all_to_all | solution.py:25
  237.1 0.5 broadcast.115
  237.6 2.3 reduce
  239.9 0.3 reshape.88
  240.1 2.4 all-to-all-done
  242.6 1.4 reduce.1
  243.9 0.3 reshape.90
  244.3 0.1 multiply_reduce_fusion
  244.4 14.2 %psum.37 = f32[2,64]{1,0:T(2,128)S(1)} all-reduce(f32[2,64]{1,0:T(2,128)S(1)} %multiply_reduce_fusion), channel_id=1, replica_groups=mesh['chan_0'=8,'chan_1'=8,'chan_2'=2,'win'=4] {'chan_0'}, use_global_device_ids=true, to_apply=%region_5.6 | all-reduce | flops 128 | bytes 1024 | tf_op jit(solution)/shard_map/psum | solution.py:30
  258.6 14.2 %psum.38 = f32[2,64]{1,0:T(2,128)S(1)} all-reduce(f32[2,64]{1,0:T(2,128)S(1)} %psum.37), channel_id=1, replica_groups=mesh['chan_0'=8,'chan_1'=8,'chan_2'=2,'win'=4] {'chan_1'}, use_global_device_ids=true, to_apply=%region_6.7 | all-reduce | flops 128 | bytes 1024 | tf_op jit(solution)/shard_map/psum | solution.py:30
  272.9 11.0 %psum.39 = f32[2,64]{1,0:T(2,128)S(1)} all-reduce(f32[2,64]{1,0:T(2,128)S(1)} %psum.38), channel_id=1, replica_groups=mesh['chan_0'=8,'chan_1'=8,'chan_2'=2,'win'=4] {'chan_2'}, use_global_device_ids=true, to_apply=%region_7.8 | all-reduce | flops 128 | bytes 1024 | tf_op jit(solution)/shard_map/psum | solution.py:30
  283.8 0.7 fusion.14
  (13 shorter events, 0.1 us)
Async XLA Ops:
  6.5 209.7 %copy-start = (f32[200,32]{0,1:T(8,128)S(1)}, f32[200,32]{0,1:T(8,128)}, u32[]{:S(2)}) copy-start(f32[200,32]{0,1:T(8,128)} %param.8) | copy-start | bytes 76804
  6.5 5.8 %copy-start.1 = (bf16[2,8,512]{2,1,0:T(8,128)(2,1)S(1)}, bf16[2,8,512]{2,1,0:T(8,128)(2,1)}, u32[]{:S(2)}) copy-start(bf16[2,8,512]{2,1,0:T(8,128)(2,1)} %param.5) | copy-start | bytes 49156
  6.5 207.5 %all-reduce.3.cloned.1.call-start = ((), (), s32[]{:S(2)}) async-start(), calls=%async_computation.2 | async-start | bytes 2097152 | tf_op jit(solution)/shard_map/psum | solution.py:15
  214.0 2.2 copy-start.2
  224.0 9.6 %all-to-all-start.1 = ((f32[4,1,16384]{2,1,0:T(1,128)}), f32[4,1,16384]{2,1,0:T(1,128)}, u32[]{:S(2)}, u32[]{:S(2)}) async-start(f32[4,1,16384]{2,1,0:T(1,128)} %reshape.87), calls=%async_computation.1 | async-start | bytes 524288 | tf_op jit(solution)/shard_map/all_to_all | solution.py:25
  233.6 8.9 %all-to-all-start = ((f32[4,1,16384]{2,1,0:T(1,128)}), f32[4,1,16384]{2,1,0:T(1,128)S(1)}, u32[]{:S(2)}, u32[]{:S(2)}) async-start(f32[4,1,16384]{2,1,0:T(1,128)} %reshape.89), calls=%async_computation | async-start | bytes 524288 | tf_op jit(solution)/shard_map/all_to_all | solution.py:25
Sparse Core Ops, SparseCore 0:
  11.6 202.4 all-reduce.2
where the time goes:
time: 292 us; the launch traced here: 291 us
  waiting for transfers between devices  204 us (70%)
  blocking collectives  39.5 us (14%)
  between operations  14.9 us (5%)
  local copies, waits for them, and re-layouts  10 us (3%)
  other arithmetic  8.76 us (3%)
  starting transfers between devices  7.45 us (3%)
  matrix products  7.18 us (2%)
    psum x1, waiting for transfers between devices, from_root(): return lax.psum(block, axis)  200 us
    psum x3, blocking collectives, over_axes(): return functools.reduce(lax.psum, axes, shard)  39.5 us
    all_to_all x2, starting transfers between devices, sum_at_owner(): lax.all_to_all(blocks, axis, split_axis=0, concat_axis=0, tiled=True)  7.45 us
  transfers between devices with their start and end apart: 3, of which 3 were waited for; matrix products, arithmetic and copies ran while one was open for 3% of the time, Pallas kernels for 0%

commit v1 on v0

v1 whole, which is shorter than its diff:
```python
import functools
import math

import jax
import jax.numpy as jnp
import numpy as np
from jax import lax
from jax.experimental import pallas as pl
from jax.experimental.pallas import tpu as pltpu
from jax.sharding import PartitionSpec as P

MESH = pl.DeviceIdType.MESH
RING = 8
ROWS = 4
DIRS = ((1, 0), (0, 1), (-1, 0), (0, -1))
TREE = (
    (2, 2, 2, 2, 2, 2, 2, 2),
    (-1, 1, 1, 1, 1, 1, 3, 3),
    (0, 1, 1, 2, 2, 2, 2, 1),
    (0, 0, 0, 1, 3, 3, 3, 3),
    (0, 0, 0, 1, 1, 0, 3, 3),
    (0, 0, 0, 0, 0, 0, 0, 1),
    (0, 0, 3, 2, 3, 3, 2, 1),
    (2, 0, 3, 2, 0, 0, 2, 0),
)
HOPS = 8
CHUNKS = 8
LAG = 4
SLOTS = CHUNKS + (HOPS - 1) * LAG
SLABS = (0, 1, 3, 2)


def turn(node, times):
    for _ in range(times % 4):
        node = ((-node[1]) % RING, node[0])
    return node


def step_from(node, direction):
    return tuple((node[i] + DIRS[direction][i]) % RING for i in range(2))


def tree_tables():
    def reached(tree, node):
        y, z = turn(node, -tree)
        return -1 if TREE[y][z] < 0 else (TREE[y][z] + tree) % 4

    def depth(tree, node):
        count = 0
        while (link := reached(tree, node)) >= 0:
            node = step_from(node, (link + 2) % 4)
            count += 1
        return count

    table = np.zeros((RING * RING, 8), np.int32)
    for y in range(RING):
        for z in range(RING):
            node = (y, z)
            for tree in range(4):
                link, level = reached(tree, node), depth(tree, node)
                assert level <= HOPS
                start = 0 if level == 0 else CHUNKS + link * SLOTS + (level - 1) * LAG
                table[y * RING + z, 4 + tree] = start
                for out in range(4):
                    if reached(tree, step_from(node, out)) == out:
                        table[y * RING + z, out] = 4 if level == 0 else link
    return table.reshape(-1)


def phase_table(band, lags):
    turns = np.arange(lags)[:, None] - lags // 2
    phase = (turns * np.arange(band)[None, :]) % (2 * band) * (math.pi / band)
    return np.concatenate([np.cos(phase), np.sin(phase)], axis=1).astype(np.float32)


def kernel(
    receivers_ref,
    sources_ref,
    basis_hbm,
    phase_hbm,
    coupling_ref,
    order_ref,
    table_ref,
    out_ref,
    basis_ref,
    phase_ref,
    rx_ref,
    gain_ref,
    taken_ref,
    pick_ref,
    mate_ref,
    block_ref,
    stream_ref,
    send_ref,
    rows_ref,
    result_ref,
    other_ref,
    part_ref,
    near_ref,
    line_ref,
    far_ref,
    local_sem,
    rx_send,
    rx_recv,
    gain_sem,
    one_send,
    one_recv,
    mate_sem,
    x_send,
    x_recv,
    flow_send,
    flow_recv,
    other_sem,
    near_send,
    near_recv,
    far_send,
    far_recv,
):
    chan, me_x = lax.axis_index("chan"), lax.axis_index("win")
    core = chan % 2
    me_y = chan // 2 % RING
    me_z = chan // (2 * RING)

    def at(dy, dz, which, dx=0):
        y, z = (me_y + dy) % RING, (me_z + dz) % RING
        return ((z * RING + y) * 2 + which, (me_x + dx) % ROWS)

    def remote(src, dst, send, recv, device):
        return pltpu.make_async_remote_copy(
            src_ref=src, dst_ref=dst, send_sem=send, recv_sem=recv, device_id=device, device_id_type=MESH
        )

    partner = at(0, 0, 1 - core)
    y_mates = [at(d, 0, core) for d in range(1, RING)]
    z_mates = [at(0, d, which) for which in (core, 1 - core) for d in range(1, RING)]
    x_mates = [at(0, 0, which, d) for which in (core, 1 - core) for d in range(1, ROWS)]
    links = [at(dy, dz, core) for dy, dz in DIRS]

    loads = [
        pltpu.make_async_copy(basis_hbm, basis_ref, local_sem.at[0]),
        pltpu.make_async_copy(phase_hbm, phase_ref, local_sem.at[1]),
        pltpu.make_async_copy(receivers_ref, rx_ref.at[0, core], local_sem.at[2]),
    ]
    for load in loads:
        load.start()
    barrier = pltpu.get_barrier_semaphore()
    greeted = [partner, *y_mates, *z_mates, *x_mates]
    for device in greeted:
        pl.semaphore_signal(barrier, inc=1, device_id=device, device_id_type=MESH)
    for c in range(8):
        gain_ref[core, c : c + 1, :] = jnp.full((1, 128), coupling_ref[c], jnp.float32)
    pl.semaphore_wait(barrier, len(greeted))

    ones = [
        remote(
            sources_ref.at[:, :, pl.ds(128 * link, 128)],
            taken_ref.at[link],
            one_send.at[link],
            one_recv.at[link],
            links[link],
        )
        for link in range(4)
    ]
    for copy in ones:
        copy.start()
    rx = []
    for n, (dx, flip) in enumerate((dx, flip) for flip in (0, 1) for dx in range(ROWS)):
        if n:
            rx.append(
                remote(
                    receivers_ref,
                    rx_ref.at[(ROWS - dx) % ROWS, core],
                    rx_send.at[n],
                    rx_recv.at[n],
                    at(0, 0, core if flip == 0 else 1 - core, dx),
                )
            )
    for copy in rx:
        copy.start()
    gains = remote(gain_ref.at[core], gain_ref.at[core], gain_sem.at[0], gain_sem.at[1], partner)
    gains.start()

    loads[0].wait()
    loads[1].wait()
    tables = lax.dot_general(
        basis_ref[...],
        phase_ref[...],
        (((0,), (0,)), ((), ())),
        precision=lax.Precision.HIGHEST,
        preferred_element_type=jnp.float32,
    )
    band = tables.shape[1] // 2
    cosine, sine = tables[:, :band], tables[:, band:]

    loads[2].wait()
    for copy in rx:
        copy.wait_recv()

    def project(n, carry):
        place, which = n // 2, n % 2
        pair = place // 2
        slab = jnp.where(pair == 2, 3, jnp.where(pair == 3, 2, pair))
        spectra = rx_ref[slab, which, place % 2].astype(jnp.float32)
        for c in range(8):
            real, imag = spectra[c : c + 1, :band], spectra[c : c + 1, band:]
            both = jnp.concatenate([real * cosine - imag * sine, real * sine + imag * cosine], axis=1)
            first = pl.multiple_of(which * 256 + c * 32, 32)
            rows_ref[place, pl.ds(first, 32), :] = both.astype(jnp.bfloat16)
        return carry

    lax.fori_loop(0, 2 * CHUNKS, project, 0)

    owners = [order_ref[b] for b in range(2)]
    roots = [(o // 2 % RING, o // (2 * RING), o % 2) for o in owners]
    relative = [((me_y - y + RING) % RING, (me_z - z + RING) % RING) for y, z, _ in roots]

    for copy in ones:
        copy.wait_recv()
    for b in range(2):
        kept = taken_ref[0]
        for link in range(1, 4):
            dy, dz = DIRS[link]
            here = jnp.logical_and(relative[b][0] == dy % RING, relative[b][1] == dz % RING)
            kept = jnp.where(here, taken_ref[link], kept)
        pick_ref[b] = kept
    mate = remote(pick_ref.at[1 - core], mate_ref, mate_sem.at[0], mate_sem.at[1], partner)
    mate.start()
    mate.wait_recv()
    mine = core == 0
    root_core = jnp.where(mine, roots[0][2], roots[1][2])
    block_ref[...] = jnp.where(root_core == core, pick_ref[core], mate_ref[...])

    crossings = []
    for dx in range(1, ROWS):
        place = SLABS.index((ROWS - dx) % ROWS)
        crossings.append(
            remote(
                block_ref.at[:, pl.ds(pl.multiple_of((me_x + dx) % ROWS * 64, 64), 64), :],
                stream_ref.at[pl.ds(2 * place, 2)],
                x_send.at[dx],
                x_recv.at[dx],
                at(0, 0, core, dx),
            )
        )
    for copy in crossings:
        copy.start()
    stream_ref[0:2] = block_ref[:, pl.ds(pl.multiple_of(me_x * 64, 64), 64), :]

    rel_y = jnp.where(mine, relative[0][0], relative[1][0])
    rel_z = jnp.where(mine, relative[0][1], relative[1][1])
    entry = (rel_y * RING + rel_z) * 8
    forward = [table_ref[entry + link] for link in range(4)]
    start = [table_ref[entry + 4 + tree] for tree in range(4)]

    def flow(link, slot):
        return remote(
            send_ref.at[link * SLOTS + slot],
            stream_ref.at[CHUNKS + link * SLOTS + slot],
            flow_send.at[link * SLOTS + slot],
            flow_recv.at[link * SLOTS + slot],
            links[link],
        )

    def pass_on(slot, own, came):
        heard = [stream_ref[CHUNKS + link * SLOTS + slot - LAG] for link in range(4)] if came else []
        for link in range(4):
            value = own if own is not None else heard[0]
            for n, got in enumerate(heard):
                value = jnp.where(forward[link] == n, got, value)
            send_ref[link * SLOTS + slot] = value
            flow(link, slot).start()

    for slot in range(CHUNKS):
        if slot and slot % 2 == 0:
            crossings[(ROWS - SLABS[slot // 2]) % ROWS - 1].wait_recv()
        if slot >= LAG:
            for link in range(4):
                flow(link, slot - LAG).wait_recv()
        pass_on(slot, stream_ref[slot], slot >= LAG)

    def later(slot, carry):
        for link in range(4):
            flow(link, slot - LAG).wait_recv()
        pass_on(slot, None, True)
        return carry

    lax.fori_loop(CHUNKS, SLOTS, later, 0)
    for slot in range(SLOTS - LAG, SLOTS):
        for link in range(4):
            flow(link, slot).wait_recv()

    total = jnp.zeros(result_ref.shape, jnp.float32)
    for place in range(CHUNKS):
        block = jnp.concatenate([stream_ref[start[tree] + place] for tree in range(4)], axis=1)
        total = total + lax.dot_general(
            rows_ref[place], block, (((1,), (1,)), ((), ())), preferred_element_type=jnp.float32
        )
    gains.wait()
    power = jnp.zeros((8, 64), jnp.float32)
    for c in range(16):
        piece = total[c * 32 : c * 32 + 32] * gain_ref[c // 8, c % 8 : c % 8 + 1, :64]
        result_ref[c * 32 : c * 32 + 32, :] = piece
        squared = piece * piece
        power = power + (squared[0:8] + squared[8:16] + squared[16:24] + squared[24:32])
    part_ref[...] = jnp.concatenate([power, power], axis=1)

    nears = [
        remote(part_ref, near_ref.at[d - 1], near_send.at[d - 1], near_recv.at[d - 1], y_mates[d - 1])
        for d in range(1, RING)
    ]
    for copy in nears:
        copy.start()
    other = remote(
        result_ref.at[pl.ds(pl.multiple_of((1 - core) * 256, 256), 256), :],
        other_ref,
        other_sem.at[0],
        other_sem.at[1],
        partner,
    )
    other.start()
    line = part_ref[...]
    for n, copy in enumerate(nears):
        copy.wait_recv()
        line = line + near_ref[n]
    line_ref[...] = line
    fars = []
    for flip in (0, 1):
        for d in range(RING):
            if d or flip:
                fars.append(
                    remote(
                        line_ref,
                        far_ref.at[flip * RING + d],
                        far_send.at[flip * RING + d],
                        far_recv.at[flip * RING + d],
                        at(0, d, core if flip == 0 else 1 - core),
                    )
                )
    for copy in fars:
        copy.start()

    for copy in [*ones, *rx, mate, *crossings, *nears]:
        copy.wait_send()

    def left(slot, carry):
        for link in range(4):
            flow(link, slot).wait_send()
        return carry

    lax.fori_loop(0, SLOTS, left, 0)
    other.wait()
    for copy in fars:
        copy.wait_recv()
    scale = []
    for flip in (0, 1):
        sums = line_ref[...] if flip == 0 else far_ref[RING]
        for d in range(1, RING):
            sums = sums + far_ref[flip * RING + d]
        power = jnp.sum(sums, axis=0, keepdims=True)[:, :64] / 32768.0
        scale.append(lax.rsqrt(power + 1e-05))
    out_ref[core] = result_ref[pl.ds(pl.multiple_of(core * 256, 256), 256), :] * scale[0]
    out_ref[1 - core] = other_ref[...] * scale[1]
    for copy in fars:
        copy.wait_send()


def per_device(receivers, sources, coupling, lag_basis, source_order):
    lags, basis_count = lag_basis.shape
    bf16, f32 = jnp.bfloat16, jnp.float32
    dma = pltpu.SemaphoreType.DMA
    anywhere = pl.BlockSpec(memory_space=pl.ANY)
    scalars = pl.BlockSpec(memory_space=pltpu.SMEM)
    out = pl.pallas_call(
        kernel,
        out_shape=jax.ShapeDtypeStruct((2, 256, 64), f32),
        in_specs=[anywhere] * 4 + [scalars] * 3,
        out_specs=pl.BlockSpec(memory_space=pltpu.VMEM),
        scratch_shapes=[
            pltpu.VMEM((lags, basis_count), f32),
            pltpu.VMEM((lags, 512), f32),
            pltpu.VMEM((ROWS, 2, 2, 8, 512), bf16),
            pltpu.VMEM((2, 8, 128), f32),
            pltpu.VMEM((4, 2, 256, 128), bf16),
            pltpu.VMEM((2, 2, 256, 128), bf16),
            pltpu.VMEM((2, 256, 128), bf16),
            pltpu.VMEM((2, 256, 128), bf16),
            pltpu.VMEM((CHUNKS + 4 * SLOTS, 64, 128), bf16),
            pltpu.VMEM((4 * SLOTS, 64, 128), bf16),
            pltpu.VMEM((CHUNKS, 512, 512), bf16),
            pltpu.VMEM((512, 64), f32),
            pltpu.VMEM((256, 64), f32),
            pltpu.VMEM((8, 128), f32),
            pltpu.VMEM((RING - 1, 8, 128), f32),
            pltpu.VMEM((8, 128), f32),
            pltpu.VMEM((2 * RING, 8, 128), f32),
            dma((3,)),
            dma((2 * ROWS,)),
            dma((2 * ROWS,)),
            dma((2,)),
            dma((4,)),
            dma((4,)),
            dma((2,)),
            dma((ROWS,)),
            dma((ROWS,)),
            dma((4 * SLOTS,)),
            dma((4 * SLOTS,)),
            dma((2,)),
            dma((RING - 1,)),
            dma((RING - 1,)),
            dma((2 * RING,)),
            dma((2 * RING,)),
        ],
        compiler_params=pltpu.CompilerParams(collective_id=0, has_side_effects=True),
    )(
        receivers,
        sources,
        lag_basis,
        jnp.asarray(phase_table(256, lags)),
        coupling,
        source_order,
        jnp.asarray(tree_tables()),
    )
    return out.reshape(2, 8, 32, 64)


def solution(mesh):
    return jax.shard_map(
        per_device,
        mesh=mesh,
        in_specs=(P("win", "chan", None), P("win", "chan", None), P("chan"), P(), P()),
        out_specs=P(None, "chan", None, "win"),
        check_vma=False,
    )
```

time: 292 us -> 76.3 us (0.26)
  waiting for transfers between devices: 204 us -> 0 us
  Pallas kernels: 0 us -> 72.9 us
  blocking collectives: 39.5 us -> 0 us
  between operations: 14.9 us -> 0.01 us
  other arithmetic: 8.76 us -> 0 us
  starting transfers between devices: 7.45 us -> 0 us
  matrix products: 7.18 us -> 0 us
  local copies, waits for them, and re-layouts: 10 us -> 3.17 us
    psum x1 -> x0, waiting for transfers between devices: 200 us -> none  [from_root(): return lax.psum(block, axis)]
    pallas_call x0 -> x1, Pallas kernels: none -> 72.9 us  [per_device(): pl.pallas_call(kernel, out_shape=jax.ShapeDtypeStruct((2, 256, 64), f32),...]
    psum x3 -> x0, blocking collectives: 39.5 us -> none  [over_axes(): return functools.reduce(lax.psum, axes, shard)]
    all_to_all x2 -> x0, starting transfers between devices: 7.45 us -> none  [sum_at_owner(): lax.all_to_all(blocks, axis, split_axis=0, concat_axis=0, tiled=True)]
    dot_general x4 -> x0, matrix products: 7.18 us -> none  [the longest x2 4.28 us: per_device(): jnp.einsum('wrf,wsf->rs', twisted, source_block, preferred_element_type=j...]
    reshape x4 -> x0, local copies, waits for them, and re-layouts: 4.2 us -> none  [cut_along(): return jnp.moveaxis(shard.reshape(*before, size, -1, *after), dim, 0)]
    all_to_all x2 -> x0, other arithmetic: 3.65 us -> none  [sum_at_owner(): lax.all_to_all(blocks, axis, split_axis=0, concat_axis=0, tiled=True)]
    all_to_all x2 -> x0, waiting for transfers between devices: 3.42 us -> none  [sum_at_owner(): lax.all_to_all(blocks, axis, split_axis=0, concat_axis=0, tiled=True)]
  transfers between devices with their start and end apart: 3 -> 0, of which waited for: 3 -> 0; matrix products, arithmetic and copies ran while one was open for 3% -> 0% of each run, Pallas kernels for 0% -> 0%
where the time goes in v1:
time: 76.3 us; the launch traced here: 76.1 us
  Pallas kernels  72.9 us (96%)
  local copies, waits for them, and re-layouts  3.17 us (4%)
    pallas_call x1, Pallas kernels, per_device(): pl.pallas_call(kernel, out_shape=jax.ShapeDtypeStruct((2, 256, 64), f32),...  72.9 us
    unnamed x2, local copies, waits for them, and re-layouts  3.17 us

profile of v1, /device:TPU:1, one launch (start us, length us, event | category | flops | bytes accessed | tf_op | source)
XLA Modules:
  0.0 76.1 jit_solution(4710023509236481125)
XLA Ops:
  0.0 1.5 %copy.8.basis_hbm = f32[200,32]{1,0:T(8,128)} copy(f32[200,32]{0,1:T(8,128)} %param.10) | data formatting | bytes 51200 | tf_op args[3]
  1.5 72.9 %shard_map.73 = f32[2,256,64]{2,1,0:T(8,128)} custom-call(bf16[2,8,512]{2,1,0:T(8,128)(2,1)} %receivers_ref.1, bf16[2,256,512]{2,1,0:T(8,128)(2,1)} %sources_ref.1, f32[200,32]{1,0:T(8,128)} %copy.8.basis_hbm, f32[200,512]{1,0:T(8,128)} %constant.4.clone.phase_hbm, f32[8]{0:T(128)} %coupling_ref.1, s32[2]{0:T(128)} %order_ref.1, s32[512]{0:T(512)} %constant.5.clone.table_ref), custom_call_target="tpu_custom_call" | custom-call | tf_op jit(solution)/shard_map/pallas_call | solution.py:373
  74.4 1.7 %copy.10 = f32[2,8,32,64]{3,2,1,0:T(8,128)} copy(f32[2,8,32,64]{3,2,1,0:T(8,128)} %bitcast.1) | data formatting | bytes 262144

commit v2 on v1

--- a/solution.py
+++ b/solution.py
@@ -12,21 +12,36 @@
 MESH = pl.DeviceIdType.MESH
 RING = 8
 ROWS = 4
-DIRS = ((1, 0), (0, 1), (-1, 0), (0, -1))
-TREE = (
-    (2, 2, 2, 2, 2, 2, 2, 2),
-    (-1, 1, 1, 1, 1, 1, 3, 3),
-    (0, 1, 1, 2, 2, 2, 2, 1),
-    (0, 0, 0, 1, 3, 3, 3, 3),
-    (0, 0, 0, 1, 1, 0, 3, 3),
-    (0, 0, 0, 0, 0, 0, 0, 1),
-    (0, 0, 3, 2, 3, 3, 2, 1),
-    (2, 0, 3, 2, 0, 0, 2, 0),
+TURNS = ((1, 0), (0, 1), (-1, 0), (0, -1))
+LINKS = TURNS + tuple((2 * y, 2 * z) for y, z in TURNS)
+TREES = (
+    (
+        (2, 6, 2, 2, 2, 2, 2, 2),
+        (-1, 1, 5, 5, 5, 7, 7, 3),
+        (0, 1, 4, 2, 2, 2, 0, 7),
+        (4, 3, 5, 4, 5, 4, 4, 5),
+        (0, 3, 0, 0, 0, 0, 0, 2),
+        (4, 5, 4, 4, 4, 4, 4, 3),
+        (0, 2, 0, 2, 2, 6, 0, 2),
+        (3, 6, 7, 6, 6, 5, 5, 6),
+    ),
+    (
+        (6, 1, 6, 6, 6, 6, 7, 6),
+        (2, 3, 2, 2, 1, 6, 6, 6),
+        (-1, 3, 5, 1, 5, 7, 3, 3),
+        (0, 2, 0, 0, 7, 0, 2, 0),
+        (4, 1, 4, 5, 7, 3, 7, 5),
+        (0, 0, 1, 0, 0, 0, 0, 4),
+        (4, 0, 4, 4, 4, 4, 4, 0),
+        (6, 3, 6, 1, 5, 2, 4, 4),
+    ),
 )
-HOPS = 8
+HOPS = 4
 CHUNKS = 8
-LAG = 4
+LAG = 6
 SLOTS = CHUNKS + (HOPS - 1) * LAG
+OWN = len(LINKS)
+PIECE = (2, ROWS, 32, 128)
 SLABS = (0, 1, 3, 2)
 
 
@@ -36,34 +51,35 @@
     return node
 
 
-def step_from(node, direction):
-    return tuple((node[i] + DIRS[direction][i]) % RING for i in range(2))
+def step_from(node, link, sign=1):
+    return tuple((node[i] + sign * LINKS[link][i]) % RING for i in range(2))
 
 
 def tree_tables():
     def reached(tree, node):
         y, z = turn(node, -tree)
-        return -1 if TREE[y][z] < 0 else (TREE[y][z] + tree) % 4
+        link = TREES[tree // 4][y][z]
+        return -1 if link < 0 else link // 4 * 4 + (link + tree) % 4
 
     def depth(tree, node):
         count = 0
         while (link := reached(tree, node)) >= 0:
-            node = step_from(node, (link + 2) % 4)
+            node = step_from(node, link, -1)
             count += 1
         return count
 
-    table = np.zeros((RING * RING, 8), np.int32)
+    table = np.zeros((RING * RING, 3 * OWN), np.int32)
     for y in range(RING):
         for z in range(RING):
-            node = (y, z)
-            for tree in range(4):
-                link, level = reached(tree, node), depth(tree, node)
+            row = table[y * RING + z]
+            for tree in range(OWN):
+                link, level = reached(tree, (y, z)), depth(tree, (y, z))
                 assert level <= HOPS
-                start = 0 if level == 0 else CHUNKS + link * SLOTS + (level - 1) * LAG
-                table[y * RING + z, 4 + tree] = start
-                for out in range(4):
-                    if reached(tree, step_from(node, out)) == out:
-                        table[y * RING + z, out] = 4 if level == 0 else link
+                row[OWN + tree] = 0 if level == 0 else link * HOPS + level - 1
+                row[2 * OWN + tree] = level
+                for out in range(OWN):
+                    if reached(tree, step_from((y, z), out)) == out:
+                        row[out] = OWN if level == 0 else link
     return table.reshape(-1)
 
 
@@ -81,7 +97,8 @@
     coupling_ref,
     order_ref,
     table_ref,
-    out_ref,
+    raw_hbm,
+    scale_ref,
     basis_ref,
     phase_ref,
     rx_ref,
@@ -90,7 +107,7 @@
     pick_ref,
     mate_ref,
     block_ref,
-    stream_ref,
+    own_ref,
     send_ref,
     rows_ref,
     result_ref,
@@ -115,6 +132,8 @@
     near_recv,
     far_send,
     far_recv,
+    raw_sem,
+    *came_refs,
 ):
     chan, me_x = lax.axis_index("chan"), lax.axis_index("win")
     core = chan % 2
@@ -134,7 +153,7 @@
     y_mates = [at(d, 0, core) for d in range(1, RING)]
     z_mates = [at(0, d, which) for which in (core, 1 - core) for d in range(1, RING)]
     x_mates = [at(0, 0, which, d) for which in (core, 1 - core) for d in range(1, ROWS)]
-    links = [at(dy, dz, core) for dy, dz in DIRS]
+    links = [at(dy, dz, core) for dy, dz in LINKS]
 
     loads = [
         pltpu.make_async_copy(basis_hbm, basis_ref, local_sem.at[0]),
@@ -153,13 +172,13 @@
 
     ones = [
         remote(
-            sources_ref.at[:, :, pl.ds(128 * link, 128)],
-            taken_ref.at[link],
-            one_send.at[link],
-            one_recv.at[link],
-            links[link],
+            sources_ref.at[:, :, tree // 4, :, pl.ds(128 * (tree % 4), 128)],
+            taken_ref.at[tree],
+            one_send.at[tree],
+            one_recv.at[tree],
+            links[tree],
         )
-        for link in range(4)
+        for tree in range(OWN)
     ]
     for copy in ones:
         copy.start()
@@ -185,7 +204,7 @@
     tables = lax.dot_general(
         basis_ref[...],
         phase_ref[...],
-        (((0,), (0,)), ((), ())),
+        (((1,), (0,)), ((), ())),
         precision=lax.Precision.HIGHEST,
         preferred_element_type=jnp.float32,
     )
@@ -218,10 +237,10 @@
         copy.wait_recv()
     for b in range(2):
         kept = taken_ref[0]
-        for link in range(1, 4):
-            dy, dz = DIRS[link]
+        for tree in range(1, OWN):
+            dy, dz = LINKS[tree]
             here = jnp.logical_and(relative[b][0] == dy % RING, relative[b][1] == dz % RING)
-            kept = jnp.where(here, taken_ref[link], kept)
+            kept = jnp.where(here, taken_ref[tree], kept)
         pick_ref[b] = kept
     mate = remote(pick_ref.at[1 - core], mate_ref, mate_sem.at[0], mate_sem.at[1], partner)
     mate.start()
@@ -235,8 +254,8 @@
         place = SLABS.index((ROWS - dx) % ROWS)
         crossings.append(
             remote(
-                block_ref.at[:, pl.ds(pl.multiple_of((me_x + dx) % ROWS * 64, 64), 64), :],
-                stream_ref.at[pl.ds(2 * place, 2)],
+                block_ref.at[:, (me_x + dx) % ROWS],
+                own_ref.at[pl.ds(2 * place, 2)],
                 x_send.at[dx],
                 x_recv.at[dx],
                 at(0, 0, core, dx),
@@ -244,61 +263,92 @@
         )
     for copy in crossings:
         copy.start()
-    stream_ref[0:2] = block_ref[:, pl.ds(pl.multiple_of(me_x * 64, 64), 64), :]
+    own_ref[0:2] = block_ref[:, me_x]
 
     rel_y = jnp.where(mine, relative[0][0], relative[1][0])
     rel_z = jnp.where(mine, relative[0][1], relative[1][1])
-    entry = (rel_y * RING + rel_z) * 8
-    forward = [table_ref[entry + link] for link in range(4)]
-    start = [table_ref[entry + 4 + tree] for tree in range(4)]
-
-    def flow(link, slot):
+    entry = (rel_y * RING + rel_z) * 3 * OWN
+    forward = [table_ref[entry + link] for link in range(OWN)]
+    place_of = [table_ref[entry + OWN + tree] for tree in range(OWN)]
+    level_of = [table_ref[entry + 2 * OWN + tree] for tree in range(OWN)]
+
+    def landing(link, hop, lane):
+        if isinstance(hop, int) and hop == HOPS:
+            return came_refs[LAG + lane].at[link]
+        return came_refs[lane].at[link * HOPS + hop]
+
+    def flow(link, hop, lane, leaving=False):
+        number = link * SLOTS + hop * LAG + lane
         return remote(
-            send_ref.at[link * SLOTS + slot],
-            stream_ref.at[CHUNKS + link * SLOTS + slot],
-            flow_send.at[link * SLOTS + slot],
-            flow_recv.at[link * SLOTS + slot],
+            send_ref.at[number],
+            came_refs[0].at[0] if leaving else landing(link, hop, lane),
+            flow_send.at[number],
+            flow_recv.at[number],
             links[link],
         )
 
-    def pass_on(slot, own, came):
-        heard = [stream_ref[CHUNKS + link * SLOTS + slot - LAG] for link in range(4)] if came else []
-        for link in range(4):
-            value = own if own is not None else heard[0]
+    def pass_on(hop, lane, own):
+        heard = []
+        if not (isinstance(hop, int) and hop == 0):
+            for link in range(OWN):
+                flow(link, hop - 1, lane).wait_recv()
+            heard = [came_refs[lane][link * HOPS + hop - 1] for link in range(OWN)]
+        for link in range(OWN):
+            value = heard[0] if own is None else own
             for n, got in enumerate(heard):
                 value = jnp.where(forward[link] == n, got, value)
-            send_ref[link * SLOTS + slot] = value
-            flow(link, slot).start()
+            send_ref[link * SLOTS + hop * LAG + lane] = value
+            flow(link, hop, lane).start()
 
     for slot in range(CHUNKS):
         if slot and slot % 2 == 0:
             crossings[(ROWS - SLABS[slot // 2]) % ROWS - 1].wait_recv()
-        if slot >= LAG:
-            for link in range(4):
-                flow(link, slot - LAG).wait_recv()
-        pass_on(slot, stream_ref[slot], slot >= LAG)
-
-    def later(slot, carry):
-        for link in range(4):
-            flow(link, slot - LAG).wait_recv()
-        pass_on(slot, None, True)
+        pass_on(slot // LAG, slot % LAG, own_ref[slot])
+    for lane in range(CHUNKS - LAG, LAG):
+        pass_on(1, lane, None)
+
+    def later(hop, carry):
+        for lane in range(LAG):
+            pass_on(hop, lane, None)
         return carry
 
-    lax.fori_loop(CHUNKS, SLOTS, later, 0)
-    for slot in range(SLOTS - LAG, SLOTS):
-        for link in range(4):
-            flow(link, slot).wait_recv()
-
-    total = jnp.zeros(result_ref.shape, jnp.float32)
-    for place in range(CHUNKS):
-        block = jnp.concatenate([stream_ref[start[tree] + place] for tree in range(4)], axis=1)
-        total = total + lax.dot_general(
-            rows_ref[place], block, (((1,), (1,)), ((), ())), preferred_element_type=jnp.float32
+    lax.fori_loop(2, HOPS, later, 0)
+    for lane in range(CHUNKS - LAG):
+        pass_on(HOPS, lane, None)
+
+    for chunk in range(CHUNKS):
+        late, lane = divmod(chunk, LAG)
+        for link in range(OWN):
+            if late:
+                flow(link, HOPS, lane).wait_recv()
+            elif lane >= CHUNKS - LAG:
+                flow(link, HOPS - 1, lane).wait_recv()
+        halves = []
+        for half in range(2):
+            pieces = []
+            for tree in range(4 * half, 4 * half + 4):
+                if late:
+                    last = level_of[tree] == HOPS
+                    got = came_refs[lane][place_of[tree] + jnp.where(last, 0, 1)]
+                    got = jnp.where(last, came_refs[LAG + lane][place_of[tree] // HOPS], got)
+                else:
+                    got = came_refs[lane][place_of[tree]]
+                pieces.append(jnp.where(level_of[tree] == 0, own_ref[chunk], got))
+            halves.append(jnp.concatenate(pieces, axis=1))
+        product = lax.dot_general(
+            rows_ref[chunk],
+            jnp.concatenate(halves, axis=0),
+            (((1,), (1,)), ((), ())),
+            preferred_element_type=jnp.float32,
         )
+        if chunk == 0:
+            result_ref[...] = product
+        else:
+            result_ref[...] += product
     gains.wait()
     power = jnp.zeros((8, 64), jnp.float32)
     for c in range(16):
-        piece = total[c * 32 : c * 32 + 32] * gain_ref[c // 8, c % 8 : c % 8 + 1, :64]
+        piece = result_ref[c * 32 : c * 32 + 32, :] * gain_ref[c // 8, c % 8 : c % 8 + 1, :64]
         result_ref[c * 32 : c * 32 + 32, :] = piece
         squared = piece * piece
         power = power + (squared[0:8] + squared[8:16] + squared[16:24] + squared[24:32])
@@ -343,23 +393,30 @@
         copy.wait_send()
 
     def left(slot, carry):
-        for link in range(4):
-            flow(link, slot).wait_send()
+        for link in range(OWN):
+            flow(link, 0, slot, True).wait_send()
         return carry
 
     lax.fori_loop(0, SLOTS, left, 0)
     other.wait()
+    writes = [
+        pltpu.make_async_copy(
+            result_ref.at[pl.ds(pl.multiple_of(core * 256, 256), 256), :], raw_hbm.at[core], raw_sem.at[0]
+        ),
+        pltpu.make_async_copy(other_ref, raw_hbm.at[1 - core], raw_sem.at[1]),
+    ]
+    for write in writes:
+        write.start()
     for copy in fars:
         copy.wait_recv()
-    scale = []
     for flip in (0, 1):
         sums = line_ref[...] if flip == 0 else far_ref[RING]
         for d in range(1, RING):
             sums = sums + far_ref[flip * RING + d]
         power = jnp.sum(sums, axis=0, keepdims=True)[:, :64] / 32768.0
-        scale.append(lax.rsqrt(power + 1e-05))
-    out_ref[core] = result_ref[pl.ds(pl.multiple_of(core * 256, 256), 256), :] * scale[0]
-    out_ref[1 - core] = other_ref[...] * scale[1]
+        scale_ref[core if flip == 0 else 1 - core] = lax.rsqrt(power + 1e-05)
+    for write in writes:
+        write.wait()
     for copy in fars:
         copy.wait_send()
 
@@ -370,22 +427,22 @@
     dma = pltpu.SemaphoreType.DMA
     anywhere = pl.BlockSpec(memory_space=pl.ANY)
     scalars = pl.BlockSpec(memory_space=pltpu.SMEM)
-    out = pl.pallas_call(
+    raw, scale = pl.pallas_call(
         kernel,
-        out_shape=jax.ShapeDtypeStruct((2, 256, 64), f32),
+        out_shape=(jax.ShapeDtypeStruct((2, 256, 64), f32), jax.ShapeDtypeStruct((2, 1, 64), f32)),
         in_specs=[anywhere] * 4 + [scalars] * 3,
-        out_specs=pl.BlockSpec(memory_space=pltpu.VMEM),
+        out_specs=(anywhere, pl.BlockSpec(memory_space=pltpu.VMEM)),
         scratch_shapes=[
-            pltpu.VMEM((lags, basis_count), f32),
+            pltpu.VMEM((basis_count, lags), f32),
             pltpu.VMEM((lags, 512), f32),
             pltpu.VMEM((ROWS, 2, 2, 8, 512), bf16),
             pltpu.VMEM((2, 8, 128), f32),
-            pltpu.VMEM((4, 2, 256, 128), bf16),
-            pltpu.VMEM((2, 2, 256, 128), bf16),
-            pltpu.VMEM((2, 256, 128), bf16),
-            pltpu.VMEM((2, 256, 128), bf16),
-            pltpu.VMEM((CHUNKS + 4 * SLOTS, 64, 128), bf16),
-            pltpu.VMEM((4 * SLOTS, 64, 128), bf16),
+            pltpu.VMEM((OWN, *PIECE), bf16),
+            pltpu.VMEM((2, *PIECE), bf16),
+            pltpu.VMEM(PIECE, bf16),
+            pltpu.VMEM(PIECE, bf16),
+            pltpu.VMEM((CHUNKS, 32, 128), bf16),
+            pltpu.VMEM((OWN * SLOTS, 32, 128), bf16),
             pltpu.VMEM((CHUNKS, 512, 512), bf16),
             pltpu.VMEM((512, 64), f32),
             pltpu.VMEM((256, 64), f32),
@@ -397,30 +454,33 @@
             dma((2 * ROWS,)),
             dma((2 * ROWS,)),
             dma((2,)),
-            dma((4,)),
-            dma((4,)),
+            dma((OWN,)),
+            dma((OWN,)),
             dma((2,)),
             dma((ROWS,)),
             dma((ROWS,)),
-            dma((4 * SLOTS,)),
-            dma((4 * SLOTS,)),
+            dma((OWN * SLOTS,)),
+            dma((OWN * SLOTS,)),
             dma((2,)),
             dma((RING - 1,)),
             dma((RING - 1,)),
             dma((2 * RING,)),
             dma((2 * RING,)),
+            dma((2,)),
+            *[pltpu.VMEM((OWN * HOPS, 32, 128), bf16)] * LAG,
+            *[pltpu.VMEM((OWN, 32, 128), bf16)] * (CHUNKS - LAG),
         ],
         compiler_params=pltpu.CompilerParams(collective_id=0, has_side_effects=True),
     )(
         receivers,
-        sources,
-        lag_basis,
+        sources.reshape(2, ROWS, 2, 32, 512),
+        lag_basis.T,
         jnp.asarray(phase_table(256, lags)),
         coupling,
         source_order,
         jnp.asarray(tree_tables()),
     )
-    return out.reshape(2, 8, 32, 64)
+    return raw.reshape(2, 8, 32, 64) * scale[:, None]
 
 
 def solution(mesh):

time: 76.3 us -> 63.3 us (0.83)
  Pallas kernels: 72.9 us -> 60.8 us
  local copies, waits for them, and re-layouts: 3.17 us -> 0.66 us
  other arithmetic: 0 us -> 1.67 us
    pallas_call x1, Pallas kernels: 72.9 us -> 60.8 us  [per_device(): pl.pallas_call(kernel, out_shape=(jax.ShapeDtypeStruct((2, 256, 64), f32)...]
    unnamed x2, local copies, waits for them, and re-layouts: 3.17 us -> 0.66 us
    mul x0 -> x1, other arithmetic: none -> 1.67 us  [per_device(): return raw.reshape(2, 8, 32, 64) * scale[:, None]]
where the time goes in v2:
time: 63.3 us; the launch traced here: 63.1 us
  Pallas kernels  60.8 us (96%)
  other arithmetic  1.67 us (3%)
  local copies, waits for them, and re-layouts  0.66 us (1%)
    pallas_call x1, Pallas kernels, per_device(): pl.pallas_call(kernel, out_shape=(jax.ShapeDtypeStruct((2, 256, 64), f32)...  60.8 us
    mul x1, other arithmetic, per_device(): return raw.reshape(2, 8, 32, 64) * scale[:, None]  1.67 us

profile of v2, /device:TPU:1, one launch (start us, length us, event | category | flops | bytes accessed | tf_op | source)
XLA Modules:
  0.0 63.1 jit_solution(16475181580758906432)
XLA Ops:
  0.0 60.8 %shard_map.73 = (f32[2,256,64]{2,1,0:T(8,128)}, f32[2,1,64]{2,1,0:T(1,128)}) custom-call(bf16[2,8,512]{2,1,0:T(8,128)(2,1)} %receivers_ref.1, bf16[2,4,2,32,512]{4,3,2,1,0:T(8,128)(2,1)} %bitcast.4, f32[32,200]{1,0:T(8,128)} %bitcast.6, f32[200,512]{1,0:T(8,128)} %constant.4.clone.phase_hbm, f32[8]{0:T(128)} %coupling_ref.1, s32[2]{0:T(128)} %order_ref.1, ...), custom_call_target="tpu_custom_call" | custom-call | tf_op jit(solution)/shard_map/pallas_call | solution.py:430
  60.8 0.0 copy-start
  60.8 0.7 %copy-done = f32[2,1,64]{2,1,0:T(1,128)S(1)} copy-done((f32[2,1,64]{2,1,0:T(1,128)S(1)}, f32[2,1,64]{2,1,0:T(1,128)}, u32[]{:S(2)}) %copy-start) | copy-done | bytes 536
  61.5 1.7 %broadcast_multiply_fusion = f32[2,8,32,64]{3,2,1,0:T(8,128)} fusion(f32[2,8,32,64]{3,2,1,0:T(8,128)} %bitcast.5, f32[2,64]{1,0:T(2,128)S(1)} %bitcast.7), kind=kLoop, calls=%fused_computation | loop fusion | flops 32768 | bytes 262656 | tf_op jit(solution)/shard_map/mul | solution.py:483
Async XLA Ops:
  60.8 0.7 %copy-start = (f32[2,1,64]{2,1,0:T(1,128)S(1)}, f32[2,1,64]{2,1,0:T(1,128)}, u32[]{:S(2)}) copy-start(f32[2,1,64]{2,1,0:T(1,128)} %get-tuple-element.8) | copy-start | bytes 1540

commit v3 on v2

--- a/solution.py
+++ b/solution.py
@@ -37,11 +37,11 @@
     ),
 )
 HOPS = 4
-CHUNKS = 8
+CHUNKS = 2 * ROWS
 LAG = 6
 SLOTS = CHUNKS + (HOPS - 1) * LAG
 OWN = len(LINKS)
-PIECE = (2, ROWS, 32, 128)
+PIECE = (ROWS, 32, 128)
 SLABS = (0, 1, 3, 2)
 
 
@@ -98,15 +98,13 @@
     order_ref,
     table_ref,
     raw_hbm,
-    scale_ref,
     basis_ref,
     phase_ref,
     rx_ref,
     gain_ref,
     taken_ref,
     pick_ref,
-    mate_ref,
-    block_ref,
+    both_ref,
     own_ref,
     send_ref,
     rows_ref,
@@ -116,13 +114,13 @@
     near_ref,
     line_ref,
     far_ref,
+    scale_ref,
     local_sem,
     rx_send,
     rx_recv,
     gain_sem,
     one_send,
     one_recv,
-    mate_sem,
     x_send,
     x_recv,
     flow_send,
@@ -172,12 +170,13 @@
 
     ones = [
         remote(
-            sources_ref.at[:, :, tree // 4, :, pl.ds(128 * (tree % 4), 128)],
-            taken_ref.at[tree],
-            one_send.at[tree],
-            one_recv.at[tree],
+            sources_ref.at[half, :, tree // 4, :, pl.ds(128 * (tree % 4), 128)],
+            taken_ref.at[half, tree],
+            one_send.at[half * OWN + tree],
+            one_recv.at[half * OWN + tree],
             links[tree],
         )
+        for half in range(2)
         for tree in range(OWN)
     ]
     for copy in ones:
@@ -217,9 +216,9 @@
 
     def project(n, carry):
         place, which = n // 2, n % 2
-        pair = place // 2
-        slab = jnp.where(pair == 2, 3, jnp.where(pair == 3, 2, pair))
-        spectra = rx_ref[slab, which, place % 2].astype(jnp.float32)
+        turned = place % ROWS
+        slab = jnp.where(turned == 2, 3, jnp.where(turned == 3, 2, turned))
+        spectra = rx_ref[slab, which, place // ROWS].astype(jnp.float32)
         for c in range(8):
             real, imag = spectra[c : c + 1, :band], spectra[c : c + 1, band:]
             both = jnp.concatenate([real * cosine - imag * sine, real * sine + imag * cosine], axis=1)
@@ -233,37 +232,34 @@
     roots = [(o // 2 % RING, o // (2 * RING), o % 2) for o in owners]
     relative = [((me_y - y + RING) % RING, (me_z - z + RING) % RING) for y, z, _ in roots]
 
-    for copy in ones:
-        copy.wait_recv()
-    for b in range(2):
-        kept = taken_ref[0]
-        for tree in range(1, OWN):
-            dy, dz = LINKS[tree]
-            here = jnp.logical_and(relative[b][0] == dy % RING, relative[b][1] == dz % RING)
-            kept = jnp.where(here, taken_ref[tree], kept)
-        pick_ref[b] = kept
-    mate = remote(pick_ref.at[1 - core], mate_ref, mate_sem.at[0], mate_sem.at[1], partner)
-    mate.start()
-    mate.wait_recv()
+    crossings = []
+    for half in range(2):
+        for tree in range(OWN):
+            ones[half * OWN + tree].wait_recv()
+        for b in range(2):
+            kept = taken_ref[half, 0]
+            for tree in range(1, OWN):
+                dy, dz = LINKS[tree]
+                here = jnp.logical_and(relative[b][0] == dy % RING, relative[b][1] == dz % RING)
+                kept = jnp.where(here, taken_ref[half, tree], kept)
+            pick_ref[half, b] = kept
+        for n in range(1, 2 * ROWS):
+            flip, dx = divmod(n, ROWS)
+            which = core if flip == 0 else 1 - core
+            place = half * ROWS + SLABS.index((ROWS - dx) % ROWS)
+            crossings.append(
+                remote(
+                    pick_ref.at[half, which, (me_x + dx) % ROWS],
+                    both_ref.at[core, place],
+                    x_send.at[half * 2 * ROWS + n],
+                    x_recv.at[half * 2 * ROWS + n],
+                    at(0, 0, which, dx),
+                )
+            )
+            crossings[-1].start()
+        both_ref[core, half * ROWS] = pick_ref[half, core, me_x]
     mine = core == 0
     root_core = jnp.where(mine, roots[0][2], roots[1][2])
-    block_ref[...] = jnp.where(root_core == core, pick_ref[core], mate_ref[...])
-
-    crossings = []
-    for dx in range(1, ROWS):
-        place = SLABS.index((ROWS - dx) % ROWS)
-        crossings.append(
-            remote(
-                block_ref.at[:, (me_x + dx) % ROWS],
-                own_ref.at[pl.ds(2 * place, 2)],
-                x_send.at[dx],
-                x_recv.at[dx],
-                at(0, 0, core, dx),
-            )
-        )
-    for copy in crossings:
-        copy.start()
-    own_ref[0:2] = block_ref[:, me_x]
 
     rel_y = jnp.where(mine, relative[0][0], relative[1][0])
     rel_z = jnp.where(mine, relative[0][1], relative[1][1])
@@ -301,9 +297,14 @@
             flow(link, hop, lane).start()
 
     for slot in range(CHUNKS):
-        if slot and slot % 2 == 0:
-            crossings[(ROWS - SLABS[slot // 2]) % ROWS - 1].wait_recv()
-        pass_on(slot // LAG, slot % LAG, own_ref[slot])
+        half, place = divmod(slot, ROWS)
+        dx = (ROWS - SLABS[place]) % ROWS
+        for n in (dx, ROWS + dx):
+            if n:
+                crossings[half * (2 * ROWS - 1) + n - 1].wait_recv()
+        own = jnp.where(root_core == 0, both_ref[0, slot], both_ref[1, slot])
+        own_ref[slot] = own
+        pass_on(slot // LAG, slot % LAG, own)
     for lane in range(CHUNKS - LAG, LAG):
         pass_on(1, lane, None)
 
@@ -341,17 +342,18 @@
             (((1,), (1,)), ((), ())),
             preferred_element_type=jnp.float32,
         )
+        product = product.reshape(16, 32, 64)
         if chunk == 0:
             result_ref[...] = product
         else:
             result_ref[...] += product
     gains.wait()
-    power = jnp.zeros((8, 64), jnp.float32)
+    power = jnp.zeros((32, 64), jnp.float32)
     for c in range(16):
-        piece = result_ref[c * 32 : c * 32 + 32, :] * gain_ref[c // 8, c % 8 : c % 8 + 1, :64]
-        result_ref[c * 32 : c * 32 + 32, :] = piece
-        squared = piece * piece
-        power = power + (squared[0:8] + squared[8:16] + squared[16:24] + squared[24:32])
+        piece = result_ref[c] * gain_ref[c // 8, c % 8 : c % 8 + 1, :64]
+        result_ref[c] = piece
+        power = power + piece * piece
+    power = jnp.sum(power, axis=0, keepdims=True)
     part_ref[...] = jnp.concatenate([power, power], axis=1)
 
     nears = [
@@ -361,7 +363,7 @@
     for copy in nears:
         copy.start()
     other = remote(
-        result_ref.at[pl.ds(pl.multiple_of((1 - core) * 256, 256), 256), :],
+        result_ref.at[pl.ds((1 - core) * 8, 8)],
         other_ref,
         other_sem.at[0],
         other_sem.at[1],
@@ -389,7 +391,7 @@
     for copy in fars:
         copy.start()
 
-    for copy in [*ones, *rx, mate, *crossings, *nears]:
+    for copy in [*ones, *rx, *crossings, *nears]:
         copy.wait_send()
 
     def left(slot, carry):
@@ -401,9 +403,9 @@
     other.wait()
     writes = [
         pltpu.make_async_copy(
-            result_ref.at[pl.ds(pl.multiple_of(core * 256, 256), 256), :], raw_hbm.at[core], raw_sem.at[0]
+            result_ref.at[pl.ds(core * 8, 8)], raw_hbm.at[core, pl.ds(0, 8)], raw_sem.at[0]
         ),
-        pltpu.make_async_copy(other_ref, raw_hbm.at[1 - core], raw_sem.at[1]),
+        pltpu.make_async_copy(other_ref, raw_hbm.at[1 - core, pl.ds(0, 8)], raw_sem.at[1]),
     ]
     for write in writes:
         write.start()
@@ -413,8 +415,11 @@
         sums = line_ref[...] if flip == 0 else far_ref[RING]
         for d in range(1, RING):
             sums = sums + far_ref[flip * RING + d]
-        power = jnp.sum(sums, axis=0, keepdims=True)[:, :64] / 32768.0
-        scale_ref[core if flip == 0 else 1 - core] = lax.rsqrt(power + 1e-05)
+        scale = lax.rsqrt(sums[:, :64] / 32768.0 + 1e-05)
+        scale_ref[core if flip == 0 else 1 - core] = jnp.broadcast_to(scale, (8, 64))
+    last = pltpu.make_async_copy(scale_ref, raw_hbm.at[:, 8, pl.ds(0, 8)], raw_sem.at[2])
+    last.start()
+    writes.append(last)
     for write in writes:
         write.wait()
     for copy in fars:
@@ -427,38 +432,37 @@
     dma = pltpu.SemaphoreType.DMA
     anywhere = pl.BlockSpec(memory_space=pl.ANY)
     scalars = pl.BlockSpec(memory_space=pltpu.SMEM)
-    raw, scale = pl.pallas_call(
+    raw = pl.pallas_call(
         kernel,
-        out_shape=(jax.ShapeDtypeStruct((2, 256, 64), f32), jax.ShapeDtypeStruct((2, 1, 64), f32)),
+        out_shape=jax.ShapeDtypeStruct((2, 9, 32, 64), f32),
         in_specs=[anywhere] * 4 + [scalars] * 3,
-        out_specs=(anywhere, pl.BlockSpec(memory_space=pltpu.VMEM)),
+        out_specs=anywhere,
         scratch_shapes=[
             pltpu.VMEM((basis_count, lags), f32),
             pltpu.VMEM((lags, 512), f32),
             pltpu.VMEM((ROWS, 2, 2, 8, 512), bf16),
             pltpu.VMEM((2, 8, 128), f32),
-            pltpu.VMEM((OWN, *PIECE), bf16),
-            pltpu.VMEM((2, *PIECE), bf16),
-            pltpu.VMEM(PIECE, bf16),
-            pltpu.VMEM(PIECE, bf16),
+            pltpu.VMEM((2, OWN, *PIECE), bf16),
+            pltpu.VMEM((2, 2, *PIECE), bf16),
+            pltpu.VMEM((2, CHUNKS, 32, 128), bf16),
             pltpu.VMEM((CHUNKS, 32, 128), bf16),
             pltpu.VMEM((OWN * SLOTS, 32, 128), bf16),
             pltpu.VMEM((CHUNKS, 512, 512), bf16),
-            pltpu.VMEM((512, 64), f32),
-            pltpu.VMEM((256, 64), f32),
-            pltpu.VMEM((8, 128), f32),
-            pltpu.VMEM((RING - 1, 8, 128), f32),
-            pltpu.VMEM((8, 128), f32),
-            pltpu.VMEM((2 * RING, 8, 128), f32),
+            pltpu.VMEM((16, 32, 64), f32),
+            pltpu.VMEM((8, 32, 64), f32),
+            pltpu.VMEM((1, 128), f32),
+            pltpu.VMEM((RING - 1, 1, 128), f32),
+            pltpu.VMEM((1, 128), f32),
+            pltpu.VMEM((2 * RING, 1, 128), f32),
+            pltpu.VMEM((2, 8, 64), f32),
             dma((3,)),
             dma((2 * ROWS,)),
             dma((2 * ROWS,)),
             dma((2,)),
-            dma((OWN,)),
-            dma((OWN,)),
-            dma((2,)),
-            dma((ROWS,)),
-            dma((ROWS,)),
+            dma((2 * OWN,)),
+            dma((2 * OWN,)),
+            dma((4 * ROWS,)),
+            dma((4 * ROWS,)),
             dma((OWN * SLOTS,)),
             dma((OWN * SLOTS,)),
             dma((2,)),
@@ -466,7 +470,7 @@
             dma((RING - 1,)),
             dma((2 * RING,)),
             dma((2 * RING,)),
-            dma((2,)),
+            dma((3,)),
             *[pltpu.VMEM((OWN * HOPS, 32, 128), bf16)] * LAG,
             *[pltpu.VMEM((OWN, 32, 128), bf16)] * (CHUNKS - LAG),
         ],
@@ -480,7 +484,7 @@
         source_order,
         jnp.asarray(tree_tables()),
     )
-    return raw.reshape(2, 8, 32, 64) * scale[:, None]
+    return raw[:, :8] * raw[:, 8:, :1]
 
 
 def solution(mesh):

time: 63.3 us -> 62.4 us (0.986)
  Pallas kernels: 60.8 us -> 59.8 us
    pallas_call x1, Pallas kernels: 60.8 us -> 59.8 us  [per_device(): pl.pallas_call(kernel, out_shape=jax.ShapeDtypeStruct((2, 9, 32, 64), f32...]
    slice x0 -> x1, local copies, waits for them, and re-layouts: none -> 0.7 us  [per_device(): return raw[:, :8] * raw[:, 8:, :1]]
    unnamed x2 -> x0, local copies, waits for them, and re-layouts: 0.66 us -> none
where the time goes in v3:
time: 62.4 us; the launch traced here: 62.2 us
  Pallas kernels  59.8 us (96%)
  other arithmetic  1.67 us (3%)
  local copies, waits for them, and re-layouts  0.7 us (1%)
    pallas_call x1, Pallas kernels, per_device(): pl.pallas_call(kernel, out_shape=jax.ShapeDtypeStruct((2, 9, 32, 64), f32...  59.8 us
    mul x1, other arithmetic, per_device(): return raw[:, :8] * raw[:, 8:, :1]  1.67 us

profile of v3, /device:TPU:1, one launch (start us, length us, event | category | flops | bytes accessed | tf_op | source)
XLA Modules:
  0.0 62.2 jit_solution(5518154501552801562)
XLA Ops:
  0.0 59.8 %shard_map.73 = f32[2,9,32,64]{3,2,1,0:T(8,128)} custom-call(bf16[2,8,512]{2,1,0:T(8,128)(2,1)} %receivers_ref.1, bf16[2,4,2,32,512]{4,3,2,1,0:T(8,128)(2,1)} %bitcast.3, f32[32,200]{1,0:T(8,128)} %bitcast.4, f32[200,512]{1,0:T(8,128)} %constant.4.clone.phase_hbm, f32[8]{0:T(128)} %coupling_ref.1, s32[2]{0:T(128)} %order_ref.1, s32[1536]{0:T(1024)} %constant.5.clone.table_ref), custom_call_target="tpu_custom_call" | custom-call | tf_op jit(solution)/shard_map/pallas_call | solution.py:435
  59.8 0.7 %slice.7 = f32[2,1,1,64]{3,2,1,0:T(1,128)S(1)} slice(f32[2,9,32,64]{3,2,1,0:T(8,128)} %shard_map.73), slice={[0:2], [8:9], [0:1], [0:64]} | slice | bytes 1024 | tf_op jit(solution)/shard_map/slice | solution.py:487
  60.5 1.7 %slice_multiply_fusion = f32[2,8,32,64]{3,2,1,0:T(8,128)} fusion(f32[2,9,32,64]{3,2,1,0:T(8,128)} %shard_map.73, f32[2,64]{1,0:T(2,128)S(1)} %bitcast.5), kind=kLoop, calls=%fused_computation | loop fusion | flops 32768 | bytes 262656 | tf_op jit(solution)/shard_map/mul | solution.py:487

commit v4 on v3

--- a/solution.py
+++ b/solution.py
@@ -94,10 +94,13 @@
     sources_ref,
     basis_hbm,
     phase_hbm,
+    coupling_hbm,
+    order_hbm,
+    table_hbm,
+    out_ref,
     coupling_ref,
     order_ref,
     table_ref,
-    raw_hbm,
     basis_ref,
     phase_ref,
     rx_ref,
@@ -111,10 +114,9 @@
     result_ref,
     other_ref,
     part_ref,
-    near_ref,
-    line_ref,
-    far_ref,
-    scale_ref,
+    plane_ref,
+    sum_ref,
+    mate_ref,
     local_sem,
     rx_send,
     rx_recv,
@@ -126,11 +128,9 @@
     flow_send,
     flow_recv,
     other_sem,
-    near_send,
-    near_recv,
-    far_send,
-    far_recv,
-    raw_sem,
+    plane_send,
+    plane_recv,
+    mate_sem,
     *came_refs,
 ):
     chan, me_x = lax.axis_index("chan"), lax.axis_index("win")
@@ -148,8 +148,6 @@
         )
 
     partner = at(0, 0, 1 - core)
-    y_mates = [at(d, 0, core) for d in range(1, RING)]
-    z_mates = [at(0, d, which) for which in (core, 1 - core) for d in range(1, RING)]
     x_mates = [at(0, 0, which, d) for which in (core, 1 - core) for d in range(1, ROWS)]
     links = [at(dy, dz, core) for dy, dz in LINKS]
 
@@ -157,15 +155,16 @@
         pltpu.make_async_copy(basis_hbm, basis_ref, local_sem.at[0]),
         pltpu.make_async_copy(phase_hbm, phase_ref, local_sem.at[1]),
         pltpu.make_async_copy(receivers_ref, rx_ref.at[0, core], local_sem.at[2]),
+        pltpu.make_async_copy(coupling_hbm, coupling_ref, local_sem.at[3]),
+        pltpu.make_async_copy(order_hbm, order_ref, local_sem.at[4]),
+        pltpu.make_async_copy(table_hbm, table_ref, local_sem.at[5]),
     ]
     for load in loads:
         load.start()
     barrier = pltpu.get_barrier_semaphore()
-    greeted = [partner, *y_mates, *z_mates, *x_mates]
+    greeted = [partner, *links, *x_mates]
     for device in greeted:
         pl.semaphore_signal(barrier, inc=1, device_id=device, device_id_type=MESH)
-    for c in range(8):
-        gain_ref[core, c : c + 1, :] = jnp.full((1, 128), coupling_ref[c], jnp.float32)
     pl.semaphore_wait(barrier, len(greeted))
 
     ones = [
@@ -195,6 +194,9 @@
             )
     for copy in rx:
         copy.start()
+    loads[3].wait()
+    for c in range(8):
+        gain_ref[core, c : c + 1, :] = jnp.full((1, 128), coupling_ref[c], jnp.float32)
     gains = remote(gain_ref.at[core], gain_ref.at[core], gain_sem.at[0], gain_sem.at[1], partner)
     gains.start()
 
@@ -228,6 +230,8 @@
 
     lax.fori_loop(0, 2 * CHUNKS, project, 0)
 
+    loads[4].wait()
+    loads[5].wait()
     owners = [order_ref[b] for b in range(2)]
     roots = [(o // 2 % RING, o // (2 * RING), o % 2) for o in owners]
     relative = [((me_y - y + RING) % RING, (me_z - z + RING) % RING) for y, z, _ in roots]
@@ -356,12 +360,21 @@
     power = jnp.sum(power, axis=0, keepdims=True)
     part_ref[...] = jnp.concatenate([power, power], axis=1)
 
-    nears = [
-        remote(part_ref, near_ref.at[d - 1], near_send.at[d - 1], near_recv.at[d - 1], y_mates[d - 1])
-        for d in range(1, RING)
-    ]
-    for copy in nears:
-        copy.start()
+    def total(n):
+        return remote(
+            part_ref,
+            plane_ref.at[pl.ds(n, 1)],
+            plane_send.at[n],
+            plane_recv.at[n],
+            at(n // RING, n % RING, core),
+        )
+
+    def start(n, carry):
+        total(n).start()
+        return carry
+
+    lax.fori_loop(1, RING * RING, start, 0)
+    plane_ref[0:1, :] = part_ref[...]
     other = remote(
         result_ref.at[pl.ds((1 - core) * 8, 8)],
         other_ref,
@@ -370,28 +383,8 @@
         partner,
     )
     other.start()
-    line = part_ref[...]
-    for n, copy in enumerate(nears):
-        copy.wait_recv()
-        line = line + near_ref[n]
-    line_ref[...] = line
-    fars = []
-    for flip in (0, 1):
-        for d in range(RING):
-            if d or flip:
-                fars.append(
-                    remote(
-                        line_ref,
-                        far_ref.at[flip * RING + d],
-                        far_send.at[flip * RING + d],
-                        far_recv.at[flip * RING + d],
-                        at(0, d, core if flip == 0 else 1 - core),
-                    )
-                )
-    for copy in fars:
-        copy.start()
-
-    for copy in [*ones, *rx, *crossings, *nears]:
+
+    for copy in [*ones, *rx, *crossings]:
         copy.wait_send()
 
     def left(slot, carry):
@@ -401,29 +394,28 @@
 
     lax.fori_loop(0, SLOTS, left, 0)
     other.wait()
-    writes = [
-        pltpu.make_async_copy(
-            result_ref.at[pl.ds(core * 8, 8)], raw_hbm.at[core, pl.ds(0, 8)], raw_sem.at[0]
-        ),
-        pltpu.make_async_copy(other_ref, raw_hbm.at[1 - core, pl.ds(0, 8)], raw_sem.at[1]),
-    ]
-    for write in writes:
-        write.start()
-    for copy in fars:
-        copy.wait_recv()
-    for flip in (0, 1):
-        sums = line_ref[...] if flip == 0 else far_ref[RING]
-        for d in range(1, RING):
-            sums = sums + far_ref[flip * RING + d]
-        scale = lax.rsqrt(sums[:, :64] / 32768.0 + 1e-05)
-        scale_ref[core if flip == 0 else 1 - core] = jnp.broadcast_to(scale, (8, 64))
-    last = pltpu.make_async_copy(scale_ref, raw_hbm.at[:, 8, pl.ds(0, 8)], raw_sem.at[2])
-    last.start()
-    writes.append(last)
-    for write in writes:
-        write.wait()
-    for copy in fars:
-        copy.wait_send()
+
+    def arrived(n, carry):
+        total(n).wait()
+        return carry
+
+    lax.fori_loop(1, RING * RING, arrived, 0)
+    sum_ref[...] = jnp.sum(plane_ref[...], axis=0, keepdims=True)
+    mate = remote(sum_ref, mate_ref, mate_sem.at[0], mate_sem.at[1], partner)
+    mate.start()
+
+    def scale(ref):
+        return lax.rsqrt(ref[:, :64] / 32768.0 + 1e-05)
+
+    out_ref[core] = result_ref[pl.ds(core * 8, 8)] * scale(sum_ref)
+    mate.wait()
+    out_ref[1 - core] = other_ref[...] * scale(mate_ref)
+
+
+def put_out(result_ref, out_ref, sem):
+    copy = pltpu.make_async_copy(result_ref, out_ref, sem)
+    copy.start()
+    copy.wait()
 
 
 def per_device(receivers, sources, coupling, lag_basis, source_order):
@@ -431,13 +423,15 @@
     bf16, f32 = jnp.bfloat16, jnp.float32
     dma = pltpu.SemaphoreType.DMA
     anywhere = pl.BlockSpec(memory_space=pl.ANY)
-    scalars = pl.BlockSpec(memory_space=pltpu.SMEM)
-    raw = pl.pallas_call(
+    result = pl.pallas_call(
         kernel,
-        out_shape=jax.ShapeDtypeStruct((2, 9, 32, 64), f32),
-        in_specs=[anywhere] * 4 + [scalars] * 3,
-        out_specs=anywhere,
+        out_shape=pltpu.VMEM((2, 8, 32, 64), f32),
+        in_specs=[anywhere] * 7,
+        out_specs=pl.BlockSpec(memory_space=pltpu.VMEM),
         scratch_shapes=[
+            pltpu.SMEM(coupling.shape, f32),
+            pltpu.SMEM(source_order.shape, jnp.int32),
+            pltpu.SMEM((RING * RING * 3 * OWN,), jnp.int32),
             pltpu.VMEM((basis_count, lags), f32),
             pltpu.VMEM((lags, 512), f32),
             pltpu.VMEM((ROWS, 2, 2, 8, 512), bf16),
@@ -451,11 +445,10 @@
             pltpu.VMEM((16, 32, 64), f32),
             pltpu.VMEM((8, 32, 64), f32),
             pltpu.VMEM((1, 128), f32),
-            pltpu.VMEM((RING - 1, 1, 128), f32),
+            pltpu.VMEM((RING * RING, 128), f32),
             pltpu.VMEM((1, 128), f32),
-            pltpu.VMEM((2 * RING, 1, 128), f32),
-            pltpu.VMEM((2, 8, 64), f32),
-            dma((3,)),
+            pltpu.VMEM((1, 128), f32),
+            dma((6,)),
             dma((2 * ROWS,)),
             dma((2 * ROWS,)),
             dma((2,)),
@@ -466,11 +459,9 @@
             dma((OWN * SLOTS,)),
             dma((OWN * SLOTS,)),
             dma((2,)),
-            dma((RING - 1,)),
-            dma((RING - 1,)),
-            dma((2 * RING,)),
-            dma((2 * RING,)),
-            dma((3,)),
+            dma((RING * RING,)),
+            dma((RING * RING,)),
+            dma((2,)),
             *[pltpu.VMEM((OWN * HOPS, 32, 128), bf16)] * LAG,
             *[pltpu.VMEM((OWN, 32, 128), bf16)] * (CHUNKS - LAG),
         ],
@@ -484,7 +475,14 @@
         source_order,
         jnp.asarray(tree_tables()),
     )
-    return raw[:, :8] * raw[:, 8:, :1]
+    return pl.pallas_call(
+        put_out,
+        out_shape=jax.ShapeDtypeStruct(result.shape, f32),
+        in_specs=[pl.BlockSpec(memory_space=pltpu.VMEM)],
+        out_specs=anywhere,
+        scratch_shapes=[dma],
+        compiler_params=pltpu.CompilerParams(vmem_limit_bytes=1 << 20),
+    )(result)
 
 
 def solution(mesh):

time: 62.4 us -> 58.6 us (0.939)
  other arithmetic: 1.67 us -> 0 us
  Pallas kernels: 59.8 us -> 58.5 us
  local copies, waits for them, and re-layouts: 0.7 us -> 0 us
    mul x1 -> x0, other arithmetic: 1.67 us -> none  [per_device(): return raw[:, :8] * raw[:, 8:, :1]]
    pallas_call x1 -> x2, Pallas kernels: 59.8 us -> 58.5 us  [the longest x1 57.8 us: per_device(): pl.pallas_call(kernel, out_shape=pltpu.VMEM((2, 8, 32, 64), f32), in_spec...]
    slice x1 -> x0, local copies, waits for them, and re-layouts: 0.7 us -> none  [per_device(): return raw[:, :8] * raw[:, 8:, :1]]
where the time goes in v4:
time: 58.6 us; the launch traced here: 58.5 us
  Pallas kernels  58.5 us (100%)
    pallas_call x1, Pallas kernels, per_device(): pl.pallas_call(kernel, out_shape=pltpu.VMEM((2, 8, 32, 64), f32), in_spec...  57.8 us

profile of v4, /device:TPU:1, one launch (start us, length us, event | category | flops | bytes accessed | tf_op | source)
XLA Modules:
  0.0 58.5 jit_solution(16538668246534541181)
XLA Ops:
  0.0 57.8 %shard_map.73.result_ref = f32[2,8,32,64]{3,2,1,0:T(8,128)S(1)} custom-call(bf16[2,8,512]{2,1,0:T(8,128)(2,1)} %receivers_ref.1, bf16[2,4,2,32,512]{4,3,2,1,0:T(8,128)(2,1)} %bitcast.2, f32[32,200]{1,0:T(8,128)} %bitcast.3, f32[200,512]{1,0:T(8,128)} %constant.4.clone.phase_hbm, f32[8]{0:T(128)} %coupling_hbm.1, s32[2]{0:T(128)} %order_hbm.1, ...), custom_call_target="tpu_custom_call" | custom-call | tf_op jit(solution)/shard_map/pallas_call | solution.py:426
  57.8 0.7 %shard_map.74 = f32[2,8,32,64]{3,2,1,0:T(8,128)} custom-call(f32[2,8,32,64]{3,2,1,0:T(8,128)S(1)} %shard_map.73.result_ref), custom_call_target="tpu_custom_call" | custom-call | tf_op jit(solution)/shard_map/pallas_call | solution.py:478

commit v5 on v4

--- a/solution.py
+++ b/solution.py
@@ -41,6 +41,11 @@
 LAG = 6
 SLOTS = CHUNKS + (HOPS - 1) * LAG
 OWN = len(LINKS)
+LONG_FIRST = (4, 5, 6, 7, 0, 1, 2, 3)
+FAR_FIRST = sorted(
+    range(1, RING * RING),
+    key=lambda n: -sum(min(d, RING - d) for d in divmod(n, RING)),
+)
 PIECE = (ROWS, 32, 128)
 SLABS = (0, 1, 3, 2)
 
@@ -178,8 +183,9 @@
         for half in range(2)
         for tree in range(OWN)
     ]
-    for copy in ones:
-        copy.start()
+    for half in range(2):
+        for tree in LONG_FIRST:
+            ones[half * OWN + tree].start()
     rx = []
     for n, (dx, flip) in enumerate((dx, flip) for flip in (0, 1) for dx in range(ROWS)):
         if n:
@@ -260,7 +266,8 @@
                     at(0, 0, which, dx),
                 )
             )
-            crossings[-1].start()
+        for n in (2, ROWS + 2, 1, 3, ROWS + 1, ROWS + 3, ROWS):
+            crossings[half * (2 * ROWS - 1) + n - 1].start()
         both_ref[core, half * ROWS] = pick_ref[half, core, me_x]
     mine = core == 0
     root_core = jnp.where(mine, roots[0][2], roots[1][2])
@@ -293,7 +300,7 @@
             for link in range(OWN):
                 flow(link, hop - 1, lane).wait_recv()
             heard = [came_refs[lane][link * HOPS + hop - 1] for link in range(OWN)]
-        for link in range(OWN):
+        for link in LONG_FIRST:
             value = heard[0] if own is None else own
             for n, got in enumerate(heard):
                 value = jnp.where(forward[link] == n, got, value)
@@ -369,11 +376,8 @@
             at(n // RING, n % RING, core),
         )
 
-    def start(n, carry):
+    for n in FAR_FIRST:
         total(n).start()
-        return carry
-
-    lax.fori_loop(1, RING * RING, start, 0)
     plane_ref[0:1, :] = part_ref[...]
     other = remote(
         result_ref.at[pl.ds((1 - core) * 8, 8)],

time: 58.6 us -> 56.8 us (0.969)
  Pallas kernels: 58.5 us -> 56.7 us
    pallas_call x1, Pallas kernels: 57.8 us -> 56 us  [per_device(): pl.pallas_call(kernel, out_shape=pltpu.VMEM((2, 8, 32, 64), f32), in_spec...]
where the time goes in v5:
time: 56.8 us; the launch traced here: 56.7 us
  Pallas kernels  56.7 us (100%)
    pallas_call x1, Pallas kernels, per_device(): pl.pallas_call(kernel, out_shape=pltpu.VMEM((2, 8, 32, 64), f32), in_spec...  56 us

profile of v5, /device:TPU:1, one launch (start us, length us, event | category | flops | bytes accessed | tf_op | source)
XLA Modules:
  0.0 56.7 jit_solution(5192550997292053726)
XLA Ops:
  0.0 56.0 %shard_map.73.result_ref = f32[2,8,32,64]{3,2,1,0:T(8,128)S(1)} custom-call(bf16[2,8,512]{2,1,0:T(8,128)(2,1)} %receivers_ref.1, bf16[2,4,2,32,512]{4,3,2,1,0:T(8,128)(2,1)} %bitcast.2, f32[32,200]{1,0:T(8,128)} %bitcast.3, f32[200,512]{1,0:T(8,128)} %constant.4.clone.phase_hbm, f32[8]{0:T(128)} %coupling_hbm.1, s32[2]{0:T(128)} %order_hbm.1, ...), custom_call_target="tpu_custom_call" | custom-call | tf_op jit(solution)/shard_map/pallas_call | solution.py:430
  56.0 0.7 %shard_map.74 = f32[2,8,32,64]{3,2,1,0:T(8,128)} custom-call(f32[2,8,32,64]{3,2,1,0:T(8,128)S(1)} %shard_map.73.result_ref), custom_call_target="tpu_custom_call" | custom-call | tf_op jit(solution)/shard_map/pallas_call | solution.py:482

commit v6 on v5

--- a/solution.py
+++ b/solution.py
@@ -47,7 +47,7 @@
     key=lambda n: -sum(min(d, RING - d) for d in divmod(n, RING)),
 )
 PIECE = (ROWS, 32, 128)
-SLABS = (0, 1, 3, 2)
+WINDOWS = ((0, 0), (0, 1), (1, 0), (3, 0), (2, 0), (1, 1), (3, 1), (2, 1))
 
 
 def turn(node, times):
@@ -164,12 +164,12 @@
         pltpu.make_async_copy(order_hbm, order_ref, local_sem.at[4]),
         pltpu.make_async_copy(table_hbm, table_ref, local_sem.at[5]),
     ]
-    for load in loads:
-        load.start()
     barrier = pltpu.get_barrier_semaphore()
     greeted = [partner, *links, *x_mates]
     for device in greeted:
         pl.semaphore_signal(barrier, inc=1, device_id=device, device_id_type=MESH)
+    for load in loads:
+        load.start()
     pl.semaphore_wait(barrier, len(greeted))
 
     ones = [
@@ -223,10 +223,10 @@
         copy.wait_recv()
 
     def project(n, carry):
-        place, which = n // 2, n % 2
-        turned = place % ROWS
-        slab = jnp.where(turned == 2, 3, jnp.where(turned == 3, 2, turned))
-        spectra = rx_ref[slab, which, place // ROWS].astype(jnp.float32)
+        slab, half, which = n // 4, n // 2 % 2, n % 2
+        place = jnp.where(slab == 1, 2, jnp.where(slab == 2, 4, 3)) + 3 * half
+        place = jnp.where(slab == 0, half, place)
+        spectra = rx_ref[slab, which, half].astype(jnp.float32)
         for c in range(8):
             real, imag = spectra[c : c + 1, :band], spectra[c : c + 1, band:]
             both = jnp.concatenate([real * cosine - imag * sine, real * sine + imag * cosine], axis=1)
@@ -256,7 +256,7 @@
         for n in range(1, 2 * ROWS):
             flip, dx = divmod(n, ROWS)
             which = core if flip == 0 else 1 - core
-            place = half * ROWS + SLABS.index((ROWS - dx) % ROWS)
+            place = WINDOWS.index(((ROWS - dx) % ROWS, half))
             crossings.append(
                 remote(
                     pick_ref.at[half, which, (me_x + dx) % ROWS],
@@ -268,7 +268,7 @@
             )
         for n in (2, ROWS + 2, 1, 3, ROWS + 1, ROWS + 3, ROWS):
             crossings[half * (2 * ROWS - 1) + n - 1].start()
-        both_ref[core, half * ROWS] = pick_ref[half, core, me_x]
+        both_ref[core, half] = pick_ref[half, core, me_x]
     mine = core == 0
     root_core = jnp.where(mine, roots[0][2], roots[1][2])
 
@@ -308,8 +308,8 @@
             flow(link, hop, lane).start()
 
     for slot in range(CHUNKS):
-        half, place = divmod(slot, ROWS)
-        dx = (ROWS - SLABS[place]) % ROWS
+        slab, half = WINDOWS[slot]
+        dx = (ROWS - slab) % ROWS
         for n in (dx, ROWS + dx):
             if n:
                 crossings[half * (2 * ROWS - 1) + n - 1].wait_recv()
@@ -356,12 +356,12 @@
         product = product.reshape(16, 32, 64)
         if chunk == 0:
             result_ref[...] = product
-        else:
+        elif chunk < CHUNKS - 1:
             result_ref[...] += product
     gains.wait()
     power = jnp.zeros((32, 64), jnp.float32)
     for c in range(16):
-        piece = result_ref[c] * gain_ref[c // 8, c % 8 : c % 8 + 1, :64]
+        piece = (result_ref[c] + product[c]) * gain_ref[c // 8, c % 8 : c % 8 + 1, :64]
         result_ref[c] = piece
         power = power + piece * piece
     power = jnp.sum(power, axis=0, keepdims=True)

time: 56.8 us -> 56.5 us (level)
  no operation moved by 1% of the time
where the time goes in v6:
time: 56.5 us; the launch traced here: 56.4 us
  Pallas kernels  56.4 us (100%)
    pallas_call x1, Pallas kernels, per_device(): pl.pallas_call(kernel, out_shape=pltpu.VMEM((2, 8, 32, 64), f32), in_spec...  55.7 us

profile of v6, /device:TPU:1, one launch (start us, length us, event | category | flops | bytes accessed | tf_op | source)
XLA Modules:
  0.0 56.4 jit_solution(16345747715310844484)
XLA Ops:
  0.0 55.7 %shard_map.73.result_ref = f32[2,8,32,64]{3,2,1,0:T(8,128)S(1)} custom-call(bf16[2,8,512]{2,1,0:T(8,128)(2,1)} %receivers_ref.1, bf16[2,4,2,32,512]{4,3,2,1,0:T(8,128)(2,1)} %bitcast.2, f32[32,200]{1,0:T(8,128)} %bitcast.3, f32[200,512]{1,0:T(8,128)} %constant.4.clone.phase_hbm, f32[8]{0:T(128)} %coupling_hbm.1, s32[2]{0:T(128)} %order_hbm.1, ...), custom_call_target="tpu_custom_call" | custom-call | tf_op jit(solution)/shard_map/pallas_call | solution.py:430
  55.7 0.7 %shard_map.74 = f32[2,8,32,64]{3,2,1,0:T(8,128)} custom-call(f32[2,8,32,64]{3,2,1,0:T(8,128)S(1)} %shard_map.73.result_ref), custom_call_target="tpu_custom_call" | custom-call | tf_op jit(solution)/shard_map/pallas_call | solution.py:482

commit v7 on v6

--- a/solution.py
+++ b/solution.py
@@ -417,9 +417,14 @@
 
 
 def put_out(result_ref, out_ref, sem):
-    copy = pltpu.make_async_copy(result_ref, out_ref, sem)
-    copy.start()
-    copy.wait()
+    copies = [
+        pltpu.make_async_copy(result_ref.at[n // 2, pl.ds(n % 2 * 4, 4)], out_ref.at[n // 2, pl.ds(n % 2 * 4, 4)], sem.at[n])
+        for n in range(4)
+    ]
+    for copy in copies:
+        copy.start()
+    for copy in copies:
+        copy.wait()
 
 
 def per_device(receivers, sources, coupling, lag_basis, source_order):
@@ -484,7 +489,7 @@
         out_shape=jax.ShapeDtypeStruct(result.shape, f32),
         in_specs=[pl.BlockSpec(memory_space=pltpu.VMEM)],
         out_specs=anywhere,
-        scratch_shapes=[dma],
+        scratch_shapes=[dma((4,))],
         compiler_params=pltpu.CompilerParams(vmem_limit_bytes=1 << 20),
     )(result)
 

time: 56.5 us -> 56.5 us (level)
  no operation moved by 1% of the time
where the time goes in v7:
time: 56.5 us; the launch traced here: 56.4 us
  Pallas kernels  56.4 us (100%)
    pallas_call x1, Pallas kernels, per_device(): pl.pallas_call(kernel, out_shape=pltpu.VMEM((2, 8, 32, 64), f32), in_spec...  55.7 us

profile of v7, /device:TPU:1, one launch (start us, length us, event | category | flops | bytes accessed | tf_op | source)
XLA Modules:
  0.0 56.4 jit_solution(8475207927681095467)
XLA Ops:
  0.0 55.7 %shard_map.73.result_ref = f32[2,8,32,64]{3,2,1,0:T(8,128)S(1)} custom-call(bf16[2,8,512]{2,1,0:T(8,128)(2,1)} %receivers_ref.1, bf16[2,4,2,32,512]{4,3,2,1,0:T(8,128)(2,1)} %bitcast.2, f32[32,200]{1,0:T(8,128)} %bitcast.3, f32[200,512]{1,0:T(8,128)} %constant.4.clone.phase_hbm, f32[8]{0:T(128)} %coupling_hbm.1, s32[2]{0:T(128)} %order_hbm.1, ...), custom_call_target="tpu_custom_call" | custom-call | tf_op jit(solution)/shard_map/pallas_call | solution.py:435
  55.7 0.7 %shard_map.74 = f32[2,8,32,64]{3,2,1,0:T(8,128)} custom-call(f32[2,8,32,64]{3,2,1,0:T(8,128)S(1)} %shard_map.73.result_ref), custom_call_target="tpu_custom_call" | custom-call | tf_op jit(solution)/shard_map/pallas_call | solution.py:487
